TPU v7x, 256 devices: a whole 4x4x8 slice. The times are simulated.
256 devices in a mesh: dp: 256 (over x, y, z, core).
Axes of the slice: x: 4, y: 4, z: 8, core: 2. Of those that a mesh axis runs over, the one named last changes fastest.
Arguments:
- bin_index: int32 [524288, 256], P('dp'), may hold values from 0 to 63
- node_ids: int32 [524288], P('dp'), may hold values from 0 to 1
- gradients: bfloat16 [524288, 32], P('dp'), may hold values from -6 to 6
- hessians: bfloat16 [524288, 32], P('dp'), may hold values from 0.02 to 0.25
Outputs:
- gains: float32 [256, 2, 64], replicated
- weights: float32 [256, 2, 64, 32], replicated
All inputs are finite; a program needn't handle non-finite values.
Results may differ from a plain program's by a relative error of at most 0.0003.
Values sent between devices are 32-bit elements; how exact they have to be, the bound alone decides.
A program may use at most 128 MiB of HBM per device.

v0:
```python
import math

import jax
import jax.numpy as jnp
from jax import lax
from jax.sharding import PartitionSpec as P

B = 64
K = 32
NODES = 2


RIDGE = 1.0


def curves(hist):
    width = hist.shape[-1] // 2
    running = jnp.cumsum(hist, axis=2)
    totals = running[:, :, -1:, :]
    right_side = totals - running

    def score(part):
        return part[..., :width] * part[..., :width] / (part[..., width:] + RIDGE)

    gains = jnp.mean(score(running) + score(right_side) - score(totals), axis=-1)
    weights = -running[..., :width] / (running[..., width:] + RIDGE)
    return (gains, weights)


def arrange(hist):
    return jnp.transpose(hist.reshape(-1, B, NODES, 2 * K), (0, 2, 1, 3))


def on_device(bin_index, node_ids, gradients, hessians):
    rows_here = bin_index.shape[0]
    features = bin_index.shape[1]
    paired = jnp.concatenate([gradients, hessians], axis=1)
    select = (node_ids[:, None] == jnp.arange(NODES, dtype=jnp.int32)[None, :]).astype(jnp.bfloat16)
    spread = (select[:, :, None] * paired[:, None, :]).reshape(rows_here, NODES * 2 * K)
    row_step = math.gcd(rows_here, 256)
    levels = jnp.arange(B, dtype=jnp.int32)
    amount = features * B

    def add_block(index, total):
        start = index * row_step
        block_bins = lax.dynamic_slice_in_dim(bin_index, start, row_step, 0)
        block_spread = lax.dynamic_slice_in_dim(spread, start, row_step, 0)
        onehot = (block_bins[:, :, None] == levels[None, None, :]).astype(jnp.bfloat16)
        onehot = onehot.reshape(row_step, amount)
        return total + lax.dot_general(
            onehot, block_spread, (((0,), (0,)), ((), ())), preferred_element_type=jnp.float32
        )

    empty = jnp.zeros((amount, NODES * 2 * K), jnp.float32)
    summed = lax.psum(lax.fori_loop(0, rows_here // row_step, add_block, empty), "dp")
    gains, weights = curves(arrange(summed))
    return (gains, weights)


def solution(mesh):
    return jax.shard_map(
        on_device,
        mesh=mesh,
        in_specs=(P("dp", None), P("dp"), P("dp", None), P("dp", None)),
        out_specs=(P(), P()),
        check_vma=False,
    )
```

profile of v0, /device:TPU:1, one launch (start us, length us, event | category | flops | bytes accessed | tf_op | source)
XLA Modules:
  0.0 474.3 jit_solution(4182197100055719353)
XLA Ops:
  7.2 0.0 all-reduce.2.cloned.1.call-start
  7.2 0.7 compare_convert_fusion
  7.9 1.0 pad_maximum_fusion
  9.0 101.4 %while.14 = (s32[]{:T(128)}, f32[16384,128]{1,0:T(8,128)}, s32[2048,256]{1,0:T(8,128)}, bf16[2048,128]{0,1:T(8,128)(2,1)S(1)}, s32[]{:T(128)}, /*index=5*/s32[]{:T(128)}, s32[]{:T(128)}, s32[]{:T(128)}) while((s32[]{:T(128)}, f32[16384,128]{1,0:T(8,128)}, s32[2048,256]{1,0:T(8,128)}, bf16[2048,128]{0,1:T(8,128)(2,1)S(1)}, ...), condition=%wide.region_1.0_spmd.clone, body=%wide.region_0.0_spmd.clone.sunk | while | flops 1082130432 | bytes 26804380 | solution.py:55
  9.0 0.1 eq.75
  9.1 1.0 constant_dynamic-slice_fusion.2
  10.1 0.1 copy.23
  10.2 2.8 bitcast_compare_fusion.2
  13.1 5.7 %convolution_add_fusion.2 = f32[16384,128]{1,0:T(8,128)} fusion(pred[256,16384]{0,1:T(32,128)(4,1)S(1)} %bitcast_compare_fusion.2, f32[16384,128]{1,0:T(8,128)} %get-tuple-element.172, pred[]{:T(512)S(6)} %compare.3, bf16[2048,128]{0,1:T(8,128)(2,1)S(1)} %get-tuple-element.182, s32[]{:T(128)S(6)} %select_n.10), kind=kOutput, calls=%fused_computation.1.clone.1 | convolution fusion | flops 1077936128 | bytes 21037060 | tf_op jit(solution)/shard_map/while/body/eval_jaxpr/dot_general | solution.py:50
  18.7 0.1 eq.75
  18.8 1.0 constant_dynamic-slice_fusion.2
  19.8 0.1 copy.23
  19.9 2.8 bitcast_compare_fusion.2
  22.8 9.0 %convolution_add_fusion.2 = f32[16384,128]{1,0:T(8,128)} fusion(pred[256,16384]{0,1:T(32,128)(4,1)S(1)} %bitcast_compare_fusion.2, f32[16384,128]{1,0:T(8,128)} %get-tuple-element.172, pred[]{:T(512)S(6)} %compare.3, bf16[2048,128]{0,1:T(8,128)(2,1)S(1)} %get-tuple-element.182, s32[]{:T(128)S(6)} %select_n.10), kind=kOutput, calls=%fused_computation.1.clone.1 | convolution fusion | flops 1077936128 | bytes 21037060 | tf_op jit(solution)/shard_map/while/body/eval_jaxpr/dot_general | solution.py:50
  31.8 0.1 eq.75
  31.9 1.0 constant_dynamic-slice_fusion.2
  32.9 0.1 copy.23
  33.0 2.8 bitcast_compare_fusion.2
  35.9 9.0 %convolution_add_fusion.2 = f32[16384,128]{1,0:T(8,128)} fusion(pred[256,16384]{0,1:T(32,128)(4,1)S(1)} %bitcast_compare_fusion.2, f32[16384,128]{1,0:T(8,128)} %get-tuple-element.172, pred[]{:T(512)S(6)} %compare.3, bf16[2048,128]{0,1:T(8,128)(2,1)S(1)} %get-tuple-element.182, s32[]{:T(128)S(6)} %select_n.10), kind=kOutput, calls=%fused_computation.1.clone.1 | convolution fusion | flops 1077936128 | bytes 21037060 | tf_op jit(solution)/shard_map/while/body/eval_jaxpr/dot_general | solution.py:50
  44.9 0.1 eq.75
  45.0 1.0 constant_dynamic-slice_fusion.2
  46.0 0.1 copy.23
  46.1 2.8 bitcast_compare_fusion.2
  48.9 9.0 %convolution_add_fusion.2 = f32[16384,128]{1,0:T(8,128)} fusion(pred[256,16384]{0,1:T(32,128)(4,1)S(1)} %bitcast_compare_fusion.2, f32[16384,128]{1,0:T(8,128)} %get-tuple-element.172, pred[]{:T(512)S(6)} %compare.3, bf16[2048,128]{0,1:T(8,128)(2,1)S(1)} %get-tuple-element.182, s32[]{:T(128)S(6)} %select_n.10), kind=kOutput, calls=%fused_computation.1.clone.1 | convolution fusion | flops 1077936128 | bytes 21037060 | tf_op jit(solution)/shard_map/while/body/eval_jaxpr/dot_general | solution.py:50
  58.0 0.1 eq.75
  58.1 1.0 constant_dynamic-slice_fusion.2
  59.1 0.1 copy.23
  59.2 2.8 bitcast_compare_fusion.2
  62.0 9.0 %convolution_add_fusion.2 = f32[16384,128]{1,0:T(8,128)} fusion(pred[256,16384]{0,1:T(32,128)(4,1)S(1)} %bitcast_compare_fusion.2, f32[16384,128]{1,0:T(8,128)} %get-tuple-element.172, pred[]{:T(512)S(6)} %compare.3, bf16[2048,128]{0,1:T(8,128)(2,1)S(1)} %get-tuple-element.182, s32[]{:T(128)S(6)} %select_n.10), kind=kOutput, calls=%fused_computation.1.clone.1 | convolution fusion | flops 1077936128 | bytes 21037060 | tf_op jit(solution)/shard_map/while/body/eval_jaxpr/dot_general | solution.py:50
  71.1 0.1 eq.75
  71.2 1.0 constant_dynamic-slice_fusion.2
  72.1 0.1 copy.23
  72.3 2.8 bitcast_compare_fusion.2
  75.1 9.0 %convolution_add_fusion.2 = f32[16384,128]{1,0:T(8,128)} fusion(pred[256,16384]{0,1:T(32,128)(4,1)S(1)} %bitcast_compare_fusion.2, f32[16384,128]{1,0:T(8,128)} %get-tuple-element.172, pred[]{:T(512)S(6)} %compare.3, bf16[2048,128]{0,1:T(8,128)(2,1)S(1)} %get-tuple-element.182, s32[]{:T(128)S(6)} %select_n.10), kind=kOutput, calls=%fused_computation.1.clone.1 | convolution fusion | flops 1077936128 | bytes 21037060 | tf_op jit(solution)/shard_map/while/body/eval_jaxpr/dot_general | solution.py:50
  84.2 0.1 eq.75
  84.3 1.0 constant_dynamic-slice_fusion.2
  85.2 0.1 copy.23
  85.4 2.8 bitcast_compare_fusion.2
  88.2 9.0 %convolution_add_fusion.2 = f32[16384,128]{1,0:T(8,128)} fusion(pred[256,16384]{0,1:T(32,128)(4,1)S(1)} %bitcast_compare_fusion.2, f32[16384,128]{1,0:T(8,128)} %get-tuple-element.172, pred[]{:T(512)S(6)} %compare.3, bf16[2048,128]{0,1:T(8,128)(2,1)S(1)} %get-tuple-element.182, s32[]{:T(128)S(6)} %select_n.10), kind=kOutput, calls=%fused_computation.1.clone.1 | convolution fusion | flops 1077936128 | bytes 21037060 | tf_op jit(solution)/shard_map/while/body/eval_jaxpr/dot_general | solution.py:50
  97.3 0.1 eq.75
  97.3 1.0 constant_dynamic-slice_fusion.2
  98.3 0.1 copy.23
  98.5 2.8 bitcast_compare_fusion.2
  101.3 9.0 %convolution_add_fusion.2 = f32[16384,128]{1,0:T(8,128)} fusion(pred[256,16384]{0,1:T(32,128)(4,1)S(1)} %bitcast_compare_fusion.2, f32[16384,128]{1,0:T(8,128)} %get-tuple-element.172, pred[]{:T(512)S(6)} %compare.3, bf16[2048,128]{0,1:T(8,128)(2,1)S(1)} %get-tuple-element.182, s32[]{:T(128)S(6)} %select_n.10), kind=kOutput, calls=%fused_computation.1.clone.1 | convolution fusion | flops 1077936128 | bytes 21037060 | tf_op jit(solution)/shard_map/while/body/eval_jaxpr/dot_general | solution.py:50
  110.3 9.0 %copy.16 = f32[16384,128]{0,1:T(8,128)} copy(f32[16384,128]{1,0:T(8,128)} %get-tuple-element.96) | data formatting | bytes 16777216 | tf_op jit(solution)/shard_map/while | solution.py:55
  119.3 13.1 %reshape.45 = f32[256,64,2,64]{1,0,3,2:T(8,128)} reshape(f32[16384,128]{0,1:T(8,128)} %copy.16) | data formatting | bytes 16777216 | tf_op jit(solution)/shard_map/reshape | solution.py:31
  132.5 0.0 all-reduce.2.cloned.1.call-update
  132.5 301.2 %all-reduce.2.cloned.1.call-done = f32[256,2,64,64]{2,0,3,1:T(8,128)} async-done(((f32[256,2,64,64]{2,0,3,1:T(8,128)}), f32[256,2,64,64]{2,0,3,1:T(8,128)}) %all-reduce.2.cloned.1.call-update) | async-done | bytes 8388624 | tf_op jit(solution)/shard_map/psum | solution.py:55
  433.7 13.7 %copy.17 = f32[256,2,64,64]{0,3,1,2:T(8,128)} copy(f32[256,2,64,64]{2,0,3,1:T(8,128)} %all-reduce.2.cloned.1.call-done) | data formatting | bytes 16777216 | tf_op jit(solution)/shard_map/psum | solution.py:55
  447.4 7.4 %fusion.10 = f32[256,2,64,64]{0,3,1,2:T(8,128)} fusion(f32[256,2,64,64]{0,3,1,2:T(8,128)} %copy.17), kind=kOutput, calls=%fused_computation.24 | output fusion | flops 132120576 | bytes 16777216 | tf_op jit(solution)/shard_map/jit(cumsum)/reduce_window_sum | solution.py:18
  454.8 0.9 fusion.9
  455.7 0.0 slice-start
  455.7 1.1 slice_bitcast_fusion
  456.7 0.0 slice-start.1
  456.8 4.5 broadcast_subtract_fusion
  461.3 0.0 slice-done
  461.3 0.5 slice-done.1
  461.8 2.6 negate_divide_fusion
  464.4 2.3 copy.19
  466.7 0.1 broadcast_multiply_fusion.1
  466.8 0.7 copy.18
  (11 shorter events, 0.1 us)
Async XLA Ops:
  7.2 426.6 %all-reduce.2.cloned.1.call-start = ((), (), s32[]{:S(2)}) async-start(), calls=%async_computation | async-start | bytes 33554432 | tf_op jit(solution)/shard_map/psum | solution.py:55
  455.7 5.6 %slice-start = ((s8[8388608]{0:T(1024)(128)(4,1)}), s8[4194304]{0:T(1024)(128)(4,1)S(1)}, s32[]{:S(2)}) async-start(s8[8388608]{0:T(1024)(128)(4,1)} %bitcast.16), calls=%async_computation.1 | async-start | bytes 8388608
  456.7 5.1 %slice-start.1 = ((s8[8388608]{0:T(1024)(128)(4,1)}), s8[4194304]{0:T(1024)(128)(4,1)S(1)}, s32[]{:S(2)}) async-start(s8[8388608]{0:T(1024)(128)(4,1)} %bitcast.16), calls=%async_computation.2 | async-start | bytes 8388608
Sparse Core Ops, SparseCore 0:
  132.6 301.0 all-reduce.1
where the time goes:
time: 476 us; the launch traced here: 474 us
  waiting for transfers between devices  301 us (63%)
  matrix products  68.8 us (14%)
  local copies, waits for them, and re-layouts  49.9 us (10%)
  other arithmetic  39.9 us (8%)
  between operations  14.1 us (3%)
    psum x1, waiting for transfers between devices, on_device(): lax.psum(lax.fori_loop(0, rows_here // row_step, add_block, empty), 'dp')  301 us
    dot_general x8, matrix products, add_block(): lax.dot_general(onehot, block_spread, (((0,), (0,)), ((), ())), preferred...  68.8 us
    eq x8, other arithmetic, add_block(): block_bins[:, :, None] == levels[None, None, :]  22.7 us
    psum x1, local copies, waits for them, and re-layouts, on_device(): lax.psum(lax.fori_loop(0, rows_here // row_step, add_block, empty), 'dp')  13.7 us
    reshape x1, local copies, waits for them, and re-layouts, arrange(): return jnp.transpose(hist.reshape(-1, B, NODES, 2 * K), (0, 2, 1, 3))  13.1 us
  transfers between devices with their start and end apart: 1, of which 1 were waited for; matrix products, arithmetic and copies ran while one was open for 0% of the time, Pallas kernels for 0%

commit v1 on v0

v1 whole, which is shorter than its diff:
```python
import functools

import jax
import jax.numpy as jnp
from jax import lax
from jax.experimental import pallas as pl
from jax.experimental.pallas import tpu as pltpu
from jax.sharding import PartitionSpec as P

MESH = pl.DeviceIdType.MESH

BINS = 64
TARGETS = 32
WIDE = 2 * TARGETS
LANES = 128
NX, NY, NZ = 4, 4, 8
PLANE = NX * NY
RIDGE = 1.0
DEPTH = 1024
ROWS_OUT = 4 * WIDE
MESSAGE = ROWS_OUT + 8
PIECE = WIDE + 8
SHARE = TARGETS + 8
PACK = 4 * TARGETS + 8


def offset(u):
    high, low = u // 2, u % 2
    return (2 + low) * (1 - high) + (1 - low) * high


def kernel(
    rows,
    bins_hbm,
    node_ref,
    grad_ref,
    hess_ref,
    weights_ref,
    gains_ref,
    bins,
    spread,
    mine,
    theirs,
    tot,
    sent,
    got,
    zsent,
    zgot,
    share,
    pack,
    mate,
    own_sem,
    pair_send,
    pair_recv,
    send_sem,
    recv_sem,
    zsend_sem,
    zrecv_sem,
    ssend_sem,
    srecv_sem,
    psend_sem,
    precv_sem,
    msend_sem,
    mrecv_sem,
):
    me = lax.axis_index("dp")
    core = me % 2
    z = (me // 2) % NZ
    y = (me // (2 * NZ)) % NY
    x = me // (2 * NZ * NY)
    sign = 1 - 2 * core
    other = 1 - core
    mate_id = me + sign

    def device(kind, a, b, zz):
        xx, yy = (b, a) if kind == 0 else (a, b)
        return ((xx * NY + yy) * NZ + zz) * 2 + core

    def place(kind):
        return (y, x) if kind == 0 else (x, y)

    def step(p, d):
        return (p + d + 8) % 4

    def remote(src, dst, send, recv, target):
        copy = pltpu.make_async_remote_copy(
            src_ref=src, dst_ref=dst, send_sem=send, recv_sem=recv, device_id=(target,), device_id_type=MESH
        )
        return copy

    own_lanes = pl.ds(pl.multiple_of(core * LANES, LANES), LANES)
    mate_lanes = pl.ds(pl.multiple_of(other * LANES, LANES), LANES)
    own_bins = pltpu.make_async_copy(bins_hbm.at[:, own_lanes], bins.at[pl.ds(0, rows)], own_sem.at[0])
    own_bins.start()

    barrier = pltpu.get_barrier_semaphore()
    greeted = [mate_id]
    for kind in (0, 1):
        a, b = place(kind)
        greeted += [device(kind, a, step(b, 1), z), device(kind, a, step(b, -1), z)]
    for d in range(1, NZ):
        greeted.append(device(0, y, x, (z + d) % NZ))
    for peer in greeted:
        pl.semaphore_signal(barrier, inc=1, device_id=(peer,), device_id_type=MESH)

    nodes = node_ref[...].astype(jnp.float32)
    grads = grad_ref[...].astype(jnp.float32)
    hesss = hess_ref[...].astype(jnp.float32)
    mine[0:TARGETS, :] = grads
    mine[TARGETS:WIDE, :] = hesss
    mine[WIDE:PIECE, :] = jnp.broadcast_to(nodes, (8, rows))

    pl.semaphore_wait(barrier, len(greeted))

    pair_bins = remote(bins_hbm.at[:, mate_lanes], bins.at[pl.ds(rows, rows)], pair_send.at[0], pair_recv.at[0], mate_id)
    pair_vals = remote(mine, theirs, pair_send.at[1], pair_recv.at[1], mate_id)
    pair_vals.start()
    pair_bins.start()

    def fill(values, start):
        which = values[WIDE : WIDE + 1, :]
        both = values[0:WIDE, :]
        for n in (0, 1):
            part = jnp.where(which == float(n), both, 0.0)
            spread[n * WIDE : (n + 1) * WIDE, start : start + rows] = part.astype(jnp.bfloat16)

    fill(mine, 0)
    pair_vals.wait_recv()
    fill(theirs, rows)
    ones = jnp.ones((8, 2 * rows), jnp.bfloat16)
    tot[...] = lax.dot_general(ones, spread[...], (((1,), (1,)), ((), ())), preferred_element_type=jnp.float32)
    own_bins.wait()
    pair_bins.wait_recv()

    def local(t, u):
        firsts = []
        for kind in (0, 1):
            a, b = place(kind)
            firsts.append(kind * 32 + step(b, offset(t) * sign) * 8 + step(a, offset(u) * sign) * 2)
        total = None
        for start in range(0, 2 * rows, DEPTH):
            block = bins[start : start + DEPTH, :]
            hot = [
                jnp.where(block <= first + j, jnp.ones((), jnp.bfloat16), jnp.zeros((), jnp.bfloat16))
                for first in firsts
                for j in (0, 1)
            ]
            term = jnp.dot(
                spread[:, start : start + DEPTH], jnp.concatenate(hot, axis=1), preferred_element_type=jnp.float32
            )
            total = term if total is None else total + term
        return total

    def message(m, kind, target):
        return remote(sent.at[m, kind], got.at[m, kind], send_sem.at[m, kind], recv_sem.at[m, kind], target)

    def arrived(m, kind):
        message(m, kind, me).wait_recv()

    def piece(total, kind, j, extra):
        value = total[:, (2 * kind + j) * LANES : (2 * kind + j + 1) * LANES]
        for m in extra:
            value = value + got[m, kind, pl.ds(j * 2 * WIDE, 2 * WIDE), :]
        return value

    def tots(kind, extra):
        value = tot[...]
        for m in extra:
            value = value + got[m, kind, pl.ds(ROWS_OUT, 8), :]
        return value

    def deliver(total, m, extra, second, d):
        for kind in (0, 1):
            for e in extra:
                arrived(e, kind)
            for j in (0, 1):
                sent[m, kind, pl.ds(j * 2 * WIDE, 2 * WIDE), :] = piece(total, kind, j, extra)
            sent[m, kind, pl.ds(ROWS_OUT, 8), :] = tots(kind, extra)
            a, b = place(kind)
            if second:
                target = device(kind, step(a, d * sign), b, z)
            else:
                target = device(kind, a, step(b, d * sign), z)
            message(m, kind, target).start()

    for t, d in ((0, 1), (1, -1), (2, 1)):

        def one(u, carry, t=t, d=d):
            deliver(local(t, u), t * 4 + u, [u] if t == 2 else [], False, d)
            return carry

        lax.fori_loop(0, 4, one, 0)

    for u, d in ((0, 1), (1, -1), (2, 1)):
        deliver(local(3, u), 12 + u, [4 + u, 8 + u] + ([12] if u == 2 else []), True, d)

    total = local(3, 3)
    for kind in (0, 1):
        extra = [7, 11, 13, 14]
        for e in extra:
            arrived(e, kind)
        for j in (0, 1):
            value = piece(total, kind, j, extra)
            for n in (0, 1):
                zsent[kind * 4 + j * 2 + n, 0:WIDE, :] = value[n * WIDE : (n + 1) * WIDE, :]
        everything = tots(kind, extra)
        for zh in range(4):
            zsent[kind * 4 + zh, WIDE:PIECE, :] = everything

    def line(d):
        to = (z + d) % NZ
        return remote(
            zsent.at[to], zgot.at[z], zsend_sem.at[to], zrecv_sem.at[z], device(0, y, x, to)
        )

    for d in (4, 3, 5, 2, 6, 1, 7):
        line(d).start()
    summed = zsent[z]
    for d in (1, 7, 2, 6, 3, 5, 4):
        source = (z + d) % NZ
        remote(zsent.at[source], zgot.at[source], zsend_sem.at[source], zrecv_sem.at[source], me).wait_recv()
        summed = summed + zgot[source]

    node = z % 2
    row_ids = lax.broadcasted_iota(jnp.int32, (WIDE, LANES), 0)
    lane_ids = lax.broadcasted_iota(jnp.int32, (WIDE, LANES), 1)
    whole = jnp.broadcast_to(summed[WIDE : WIDE + 1, :], (WIDE, LANES))
    column = jnp.sum(jnp.where(row_ids + node * WIDE == lane_ids, whole, 0.0), axis=1, keepdims=True)
    left_g, left_h = summed[0:TARGETS, :], summed[TARGETS:WIDE, :]
    all_g, all_h = column[0:TARGETS, :], column[TARGETS:WIDE, :]
    right_g, right_h = all_g - left_g, all_h - left_h
    score = (
        left_g * left_g / (left_h + RIDGE)
        + right_g * right_g / (right_h + RIDGE)
        - all_g * all_g / (all_h + RIDGE)
    )
    share[z, 0:TARGETS, :] = -left_g / (left_h + RIDGE)
    share[z, TARGETS:SHARE, :] = jnp.broadcast_to(jnp.sum(score, axis=0, keepdims=True) * (1.0 / TARGETS), (8, LANES))

    def spread_line(slot, to, target):
        return remote(share.at[slot], share.at[slot], ssend_sem.at[to], srecv_sem.at[slot], target)

    for d in (4, 3, 5, 2, 6, 1, 7):
        to = (z + d) % NZ
        spread_line(z, to, device(0, y, x, to)).start()
    for d in (1, 7, 2, 6, 3, 5, 4):
        source = (z + d) % NZ
        spread_line(source, source, me).wait_recv()

    def pass_on(kind, slot, target, k):
        remote(
            pack.at[kind, slot], pack.at[kind, slot], psend_sem.at[kind, k], precv_sem.at[kind, slot], target
        ).start()

    def landed(kind, slot):
        remote(pack.at[kind, slot], pack.at[kind, slot], psend_sem.at[kind, 0], precv_sem.at[kind, slot], me).wait_recv()

    def write(src, kind, b, lanes):
        for a in range(4):
            for j in (0, 1):
                for n in (0, 1):
                    row = n * BINS + kind * 32 + b * 8 + a * 2 + j
                    weights_ref[pl.ds(pl.multiple_of(row * TARGETS, TARGETS), TARGETS), lanes] = src[
                        kind, b * 4 + a, pl.ds((j * 2 + n) * TARGETS, TARGETS), :
                    ]
        for n in (0, 1):
            rows8 = [
                src[kind, b * 4 + a, pl.ds(4 * TARGETS + j * 2 + n, 1), :] for a in range(4) for j in (0, 1)
            ]
            start = pl.multiple_of(n * BINS + kind * 32 + b * 8, 8)
            gains_ref[pl.ds(start, 8), lanes] = jnp.concatenate(rows8, axis=0)

    def to_mate(kind, slot):
        remote(
            pack.at[kind, slot], mate.at[kind, slot], msend_sem.at[kind, slot], mrecv_sem.at[kind, slot], mate_id
        ).start()

    for kind in (0, 1):
        a, b = place(kind)
        slot = b * 4 + a
        for zh in range(4):
            pack[kind, slot, pl.ds(zh * TARGETS, TARGETS), :] = share[kind * 4 + zh, 0:TARGETS, :]
            pack[kind, slot, pl.ds(4 * TARGETS + zh, 1), :] = share[kind * 4 + zh, TARGETS : TARGETS + 1, :]
            pack[kind, slot, pl.ds(4 * TARGETS + 4 + zh, 1), :] = share[kind * 4 + zh, TARGETS : TARGETS + 1, :]
        pass_on(kind, slot, device(kind, step(a, sign), b, z), 0)
        pass_on(kind, slot, device(kind, step(a, -sign), b, z), 1)
        pass_on(kind, slot, device(kind, a, step(b, sign), z), 3)
        pass_on(kind, slot, device(kind, a, step(b, -sign), z), 4)
        to_mate(kind, slot)

    for i, d in ((1, -1), (2, 1), (3, 2)):
        for kind in (0, 1):
            a, b = place(kind)
            slot = b * 4 + step(a, d * sign)
            landed(kind, slot)
            if i == 1:
                pass_on(kind, slot, device(kind, step(a, sign), b, z), 2)
            pass_on(kind, slot, device(kind, a, step(b, sign), z), 3 + 2 * i)
            pass_on(kind, slot, device(kind, a, step(b, -sign), z), 4 + 2 * i)
            to_mate(kind, slot)

    for d2 in (-1, 1, 2):
        for i, d in ((0, 0), (1, -1), (2, 1), (3, 2)):
            for kind in (0, 1):
                a, b = place(kind)
                slot = step(b, d2 * sign) * 4 + step(a, d * sign)
                landed(kind, slot)
                if d2 == -1:
                    pass_on(kind, slot, device(kind, a, step(b, sign), z), 11 + i)
                to_mate(kind, slot)

    def finish(b, carry):
        for kind in (0, 1):
            write(pack, kind, b, own_lanes)
        return carry

    lax.fori_loop(0, 4, finish, 0)

    def finish_mate(b, carry):
        for kind in (0, 1):
            for a in range(4):
                slot = b * 4 + a
                remote(
                    mate.at[kind, slot], mate.at[kind, slot], msend_sem.at[kind, slot], mrecv_sem.at[kind, slot], me
                ).wait_recv()
            write(mate, kind, b, mate_lanes)
        return carry

    lax.fori_loop(0, 4, finish_mate, 0)

    pair_bins.wait_send()
    pair_vals.wait_send()

    def drain(m, carry):
        for kind in (0, 1):
            message(m, kind, me).wait_send()
            remote(pack.at[kind, 0], pack.at[kind, 0], psend_sem.at[kind, m], precv_sem.at[kind, 0], me).wait_send()
        return carry

    lax.fori_loop(0, 15, drain, 0)

    def drain_mate(slot, carry):
        for kind in (0, 1):
            remote(
                pack.at[kind, slot], pack.at[kind, slot], msend_sem.at[kind, slot], mrecv_sem.at[kind, slot], me
            ).wait_send()
        return carry

    lax.fori_loop(0, PLANE, drain_mate, 0)
    for d in range(1, NZ):
        to = (z + d) % NZ
        line(d).wait_send()
        spread_line(z, to, me).wait_send()


def on_device(bin_index, node_ids, gradients, hessians):
    rows, features = bin_index.shape
    dma = pltpu.SemaphoreType.DMA
    f32 = jnp.float32
    whole = pl.BlockSpec(memory_space=pltpu.VMEM)
    weights, gains = pl.pallas_call(
        functools.partial(kernel, rows),
        out_shape=(
            jax.ShapeDtypeStruct((2 * BINS * TARGETS, features), f32),
            jax.ShapeDtypeStruct((2 * BINS, features), f32),
        ),
        in_specs=[pl.BlockSpec(memory_space=pl.ANY), whole, whole, whole],
        out_specs=(whole, whole),
        scratch_shapes=[
            pltpu.VMEM((2 * rows, LANES), jnp.int32),
            pltpu.VMEM((2 * WIDE, 2 * rows), jnp.bfloat16),
            pltpu.VMEM((PIECE, rows), f32),
            pltpu.VMEM((PIECE, rows), f32),
            pltpu.VMEM((8, LANES), f32),
            pltpu.VMEM((15, 2, MESSAGE, LANES), f32),
            pltpu.VMEM((15, 2, MESSAGE, LANES), f32),
            pltpu.VMEM((NZ, PIECE, LANES), f32),
            pltpu.VMEM((NZ, PIECE, LANES), f32),
            pltpu.VMEM((NZ, SHARE, LANES), f32),
            pltpu.VMEM((2, PLANE, PACK, LANES), f32),
            pltpu.VMEM((2, PLANE, PACK, LANES), f32),
            dma((1,)),
            dma((2,)),
            dma((2,)),
            dma((15, 2)),
            dma((15, 2)),
            dma((NZ,)),
            dma((NZ,)),
            dma((NZ,)),
            dma((NZ,)),
            dma((2, 15)),
            dma((2, PLANE)),
            dma((2, PLANE)),
            dma((2, PLANE)),
        ],
        compiler_params=pltpu.CompilerParams(collective_id=0, has_side_effects=True, vmem_limit_bytes=56 << 20),
        name="level",
    )(bin_index, node_ids.reshape(1, rows), gradients.T, hessians.T)
    weights = jnp.transpose(weights.reshape(2, BINS, TARGETS, features), (3, 0, 1, 2))
    gains = jnp.transpose(gains.reshape(2, BINS, features), (2, 0, 1))
    return (gains, weights)


def solution(mesh):
    return jax.shard_map(
        on_device,
        mesh=mesh,
        in_specs=(P("dp", None), P("dp"), P("dp", None), P("dp", None)),
        out_specs=(P(), P()),
        check_vma=False,
    )
```

time: 476 us -> 85.4 us (0.18)
  waiting for transfers between devices: 301 us -> 0 us
  Pallas kernels: 0 us -> 78.2 us
  matrix products: 68.8 us -> 0 us
  local copies, waits for them, and re-layouts: 49.9 us -> 6.36 us
  other arithmetic: 39.9 us -> 0 us
  between operations: 14.1 us -> 0.64 us
    psum x1 -> x0, waiting for transfers between devices: 301 us -> none  [on_device(): lax.psum(lax.fori_loop(0, rows_here // row_step, add_block, empty), 'dp')]
    pallas_call x0 -> x1, Pallas kernels: none -> 78.2 us  [on_device(): pl.pallas_call(functools.partial(kernel, rows), out_shape=(jax.ShapeDtype...]
    dot_general x8 -> x0, matrix products: 68.8 us -> none  [add_block(): lax.dot_general(onehot, block_spread, (((0,), (0,)), ((), ())), preferred...]
    eq x8 -> x0, other arithmetic: 22.7 us -> none  [add_block(): block_bins[:, :, None] == levels[None, None, :]]
    psum x1 -> x0, local copies, waits for them, and re-layouts: 13.7 us -> none  [on_device(): lax.psum(lax.fori_loop(0, rows_here // row_step, add_block, empty), 'dp')]
    reshape x1 -> x0, local copies, waits for them, and re-layouts: 13.1 us -> none  [arrange(): return jnp.transpose(hist.reshape(-1, B, NODES, 2 * K), (0, 2, 1, 3))]
    while x1 -> x0, local copies, waits for them, and re-layouts: 9 us -> none  [on_device(): lax.fori_loop(0, rows_here // row_step, add_block, empty)]
    dynamic_slice x16 -> x0, local copies, waits for them, and re-layouts: 8.82 us -> none  [add_block(): block_bins = lax.dynamic_slice_in_dim(bin_index, start, row_step, 0)]
  transfers between devices with their start and end apart: 1 -> 0, of which waited for: 1 -> 0; matrix products, arithmetic and copies ran while one was open for 0% -> 0% of each run, Pallas kernels for 0% -> 0%
where the time goes in v1:
time: 85.4 us; the launch traced here: 85.2 us
  Pallas kernels  78.2 us (92%)
  local copies, waits for them, and re-layouts  6.36 us (7%)
    pallas_call x1, Pallas kernels, on_device(): pl.pallas_call(functools.partial(kernel, rows), out_shape=(jax.ShapeDtype...  78.2 us
    unnamed x2, local copies, waits for them, and re-layouts  6.36 us

profile of v1, /device:TPU:1, one launch (start us, length us, event | category | flops | bytes accessed | tf_op | source)
XLA Modules:
  0.0 85.2 jit_solution(4787324821735084298)
XLA Ops:
  0.6 78.2 %level.1 = (f32[4096,256]{1,0:T(8,128)}, f32[128,256]{1,0:T(8,128)}) custom-call(s32[2048,256]{1,0:T(8,128)} %bins_hbm.1, s32[1,2048]{1,0:T(1,128)} %bitcast.13, bf16[32,2048]{1,0:T(8,128)(2,1)} %bitcast.10, bf16[32,2048]{1,0:T(8,128)(2,1)} %bitcast.11), custom_call_target="tpu_custom_call" | custom-call | tf_op jit(solution)/shard_map/level/pallas_call | solution.py:361
  78.9 1.6 %copy.8 = f32[256,2,64]{0,2,1:T(8,128)} copy(f32[256,2,64]{0,2,1:T(8,128)} %bitcast.12) | data formatting | bytes 262144
  80.4 4.8 %copy.9 = f32[256,2,64,32]{0,3,2,1:T(8,128)} copy(f32[256,2,64,32]{0,3,2,1:T(8,128)} %bitcast.9) | data formatting | bytes 8388608

commit v2 on v1

v2 whole, which is shorter than its diff:
```python
import functools

import jax
import jax.numpy as jnp
from jax import lax
from jax.experimental import pallas as pl
from jax.experimental.pallas import tpu as pltpu
from jax.sharding import PartitionSpec as P

MESH = pl.DeviceIdType.MESH

BINS = 64
TARGETS = 32
WIDE = 2 * TARGETS
LANES = 128
NX, NY, NZ = 4, 4, 8
PLANE = NX * NY
RIDGE = 1.0
DEPTH = 1024
PIECE = WIDE + 8
EARLY = 3
LAG = 3
SHARE = TARGETS + 8
PACK = 4 * TARGETS + 8


def offset(u):
    high, low = u // 2, u % 2
    return (2 + low) * (1 - high) + (1 - low) * high


def kernel(
    rows,
    bins_hbm,
    node_hbm,
    grad_hbm,
    hess_hbm,
    weights_ref,
    gains_ref,
    node_ref,
    grad_ref,
    hess_ref,
    bins,
    spread,
    mine,
    theirs,
    early,
    tz,
    tline,
    raw,
    pairs,
    paired,
    sent1,
    got1,
    sent0,
    got0,
    zsent,
    zgot,
    share,
    pack,
    mate,
    own_sem,
    swap_send,
    swap_recv,
    tz_send,
    tz_recv,
    tl_send,
    tl_recv,
    pair_send,
    pair_recv,
    send1,
    recv1,
    send0,
    recv0,
    zsend,
    zrecv,
    ssend_sem,
    srecv_sem,
    psend_sem,
    precv_sem,
    msend_sem,
    mrecv_sem,
):
    me = lax.axis_index("dp")
    core = me % 2
    z = (me // 2) % NZ
    y = (me // (2 * NZ)) % NY
    x = me // (2 * NZ * NY)
    sign = 1 - 2 * core
    other = 1 - core
    mate_id = me + sign
    h = z % 2
    partners = ((z + 1 - 2 * h + NZ) % NZ, (z - 1 + 2 * h + NZ) % NZ)

    def device(kind, a, b, zz):
        xx, yy = (b, a) if kind == 0 else (a, b)
        return ((xx * NY + yy) * NZ + zz) * 2 + core

    def place(kind):
        return (y, x) if kind == 0 else (x, y)

    def step(p, d):
        return (p + d + 8) % 4

    def remote(src, dst, send, recv, target):
        return pltpu.make_async_remote_copy(
            src_ref=src, dst_ref=dst, send_sem=send, recv_sem=recv, device_id=(target,), device_id_type=MESH
        )

    own_lanes = pl.ds(pl.multiple_of(core * LANES, LANES), LANES)
    mate_lanes = pl.ds(pl.multiple_of(other * LANES, LANES), LANES)
    loads = [
        pltpu.make_async_copy(grad_hbm, grad_ref, own_sem.at[0]),
        pltpu.make_async_copy(hess_hbm, hess_ref, own_sem.at[1]),
        pltpu.make_async_copy(node_hbm, node_ref, own_sem.at[2]),
        pltpu.make_async_copy(bins_hbm.at[:, own_lanes], bins.at[pl.ds(0, rows)], own_sem.at[3]),
    ]
    for load in loads:
        load.start()

    barrier = pltpu.get_barrier_semaphore()
    greeted = [mate_id]
    for kind in (0, 1):
        a, b = place(kind)
        greeted += [device(kind, a, step(b, d), z) for d in (1, 2, 3)]
    for d in range(1, NZ):
        greeted.append(device(0, y, x, (z + d) % NZ))
    for peer in greeted:
        pl.semaphore_signal(barrier, inc=1, device_id=(peer,), device_id_type=MESH)

    for load in loads[:3]:
        load.wait()
    mine[0:TARGETS, :] = grad_ref[...].astype(jnp.float32)
    mine[TARGETS:WIDE, :] = hess_ref[...].astype(jnp.float32)
    mine[WIDE:PIECE, :] = jnp.broadcast_to(node_ref[...].astype(jnp.float32), (8, rows))

    pl.semaphore_wait(barrier, len(greeted))

    swap_vals = remote(mine, theirs, swap_send.at[1], swap_recv.at[1], mate_id)
    swap_bins = remote(bins_hbm.at[:, mate_lanes], bins.at[pl.ds(rows, rows)], swap_send.at[0], swap_recv.at[0], mate_id)
    swap_vals.start()
    swap_bins.start()

    def fill(values, start):
        which = values[WIDE : WIDE + 1, :]
        both = values[0:WIDE, :]
        for n in (0, 1):
            part = jnp.where(which == float(n), both, 0.0)
            spread[n * WIDE : (n + 1) * WIDE, start : start + rows] = part.astype(jnp.bfloat16)

    def local(i, low, high):
        t, u = i // 4, i % 4
        firsts = []
        for kind in (0, 1):
            a, b = place(kind)
            firsts.append(kind * 32 + step(b, offset(t) * sign) * 8 + step(a, offset(u) * sign) * 2)
        total = None
        for start in range(low, high, DEPTH):
            block = bins[start : start + DEPTH, :]
            hot = [
                jnp.where(block <= first + j, jnp.ones((), jnp.bfloat16), jnp.zeros((), jnp.bfloat16))
                for first in firsts
                for j in (0, 1)
            ]
            term = jnp.dot(
                spread[:, start : start + DEPTH], jnp.concatenate(hot, axis=1), preferred_element_type=jnp.float32
            )
            total = term if total is None else total + term
        return total

    def tz_copy(slot, target):
        return remote(tz.at[slot], tz.at[slot], tz_send.at[target], tz_recv.at[slot], device(0, y, x, target))

    def tl_copy(kind, slot, to):
        a, b = place(kind)
        return remote(
            tline.at[kind, slot], tline.at[kind, slot], tl_send.at[kind, to], tl_recv.at[kind, slot], device(kind, a, to, z)
        )

    def totals_begin():
        ones = jnp.ones((8, 2 * rows), jnp.bfloat16)
        tz[z] = lax.dot_general(ones, spread[...], (((1,), (1,)), ((), ())), preferred_element_type=jnp.float32)
        for d in range(1, NZ):
            tz_copy(z, (z + d) % NZ).start()

    def totals_z():
        value = tz[z]
        for d in range(1, NZ):
            source = (z + d) % NZ
            tz_copy(source, source).wait_recv()
            value = value + tz[source]
        return value

    def totals_line(kind):
        a, b = place(kind)
        value = tline[kind, b]
        for d in (1, 2, 3):
            source = step(b, d)
            tl_copy(kind, source, source).wait_recv()
            value = value + tline[kind, source]
        return value

    def totals_send(kind, value):
        a, b = place(kind)
        tline[kind, b] = value
        for d in (1, 2, 3):
            tl_copy(kind, b, step(b, d)).start()

    def one(m, kind, target):
        return remote(sent1.at[m, kind], got1.at[m, kind], send1.at[m, kind], recv1.at[m, kind], target)

    def zero(m, kind, target):
        return remote(sent0.at[m, kind], got0.at[m, kind], send0.at[m, kind], recv0.at[m, kind], target)

    def pair(i, kind):
        a, b = place(kind)
        return remote(
            pairs.at[i, kind, 1 - h],
            paired.at[i, kind],
            pair_send.at[i, kind],
            pair_recv.at[i, kind],
            device(kind, a, b, partners[kind]),
        )

    toward = (1, -1, 1)

    def extras(i):
        t, u = i // 4, i % 4
        if t < 2:
            return []
        if t == 2:
            return [u]
        return [4 + u, 8 + u] + ([12] if u == 2 else []) + ([13, 14] if u == 3 else [])

    def target_of(i, kind):
        t, u = i // 4, i % 4
        a, b = place(kind)
        if t < 3:
            return device(kind, a, step(b, toward[t] * sign), z)
        return device(kind, step(a, toward[u] * sign), b, z)

    def put1(i, kind, value):
        for e in extras(i):
            one(e, kind, me).wait_recv()
            value = value + got1[e, kind]
        if i == 15:
            for n in (0, 1):
                zsent[kind * 4 + 2 + n] = value[n * WIDE : (n + 1) * WIDE, :]
        else:
            sent1[i, kind] = value
            one(i, kind, target_of(i, kind)).start()

    def put0(i):
        for kind in (0, 1):
            pair(i, kind).wait_recv()
            value = pairs[i, kind, h] + paired[i, kind]
            for e in extras(i):
                zero(e, kind, me).wait_recv()
                value = value + got0[e, kind]
            if i == 15:
                zsent[kind * 4 + h] = value
            else:
                sent0[i, kind] = value
                zero(i, kind, target_of(i, kind)).start()

    def late1(i):
        for kind in (0, 1):
            put1(i, kind, raw[i - 12, kind])

    def take(i, total):
        for kind in (0, 1):
            first = total[:, 2 * kind * LANES : (2 * kind + 1) * LANES]
            pairs[i, kind, 0] = first[0:WIDE, :]
            pairs[i, kind, 1] = first[WIDE : 2 * WIDE, :]
            pair(i, kind).start()
            second = total[:, (2 * kind + 1) * LANES : (2 * kind + 2) * LANES]
            if i < 12:
                put1(i, kind, second)
            else:
                raw[i - 12, kind] = second

    fill(mine, 0)
    loads[3].wait()
    for i in range(EARLY):
        early[i] = local(i, 0, rows)
    swap_vals.wait_recv()
    fill(theirs, rows)
    swap_bins.wait_recv()

    for i in range(16):
        if i < EARLY:
            take(i, early[i] + local(i, rows, 2 * rows))
        else:
            take(i, local(i, 0, 2 * rows))
        if i == 1:
            totals_begin()
        if i == 5:
            totals_send(0, totals_z())
        if i == 9:
            totals_send(1, totals_line(0))
        if LAG <= i:
            if i - LAG < 12:
                put0(i - LAG)
        if i == 13:
            late1(12)
        if i == 14:
            late1(13)
    put0(12)
    late1(14)
    put0(13)
    put0(14)
    late1(15)

    def line(to):
        return remote(zsent.at[to], zgot.at[z], zsend.at[to], zrecv.at[z], device(0, y, x, to))

    def wide(zz):
        return (zz // 2) % 2 == 1

    for d in (4, 3, 5, 2, 6, 1, 7):
        to = (z + d) % NZ

        @pl.when(wide(to))
        def _(to=to):
            line(to).start()

    put0(15)
    for d in (4, 2, 6):
        to = (z + d) % NZ

        @pl.when(jnp.logical_not(wide(to)))
        def _(to=to):
            line(to).start()

    everything = totals_line(1)

    def come(d):
        source = (z + d) % NZ
        remote(zsent.at[source], zgot.at[source], zsend.at[source], zrecv.at[source], me).wait_recv()
        return zgot[source]

    @pl.when(wide(z))
    def _():
        value = zsent[z]
        for d in (1, 7, 3, 5):
            value = value + come(d)
        zsent[z] = value

    summed = zsent[z]
    for d in (2, 6, 4):
        summed = summed + come(d)

    row_ids = lax.broadcasted_iota(jnp.int32, (WIDE, LANES), 0)
    lane_ids = lax.broadcasted_iota(jnp.int32, (WIDE, LANES), 1)
    whole = jnp.broadcast_to(everything[0:1, :], (WIDE, LANES))
    column = jnp.sum(jnp.where(row_ids + h * WIDE == lane_ids, whole, 0.0), axis=1, keepdims=True)
    left_g, left_h = summed[0:TARGETS, :], summed[TARGETS:WIDE, :]
    all_g, all_h = column[0:TARGETS, :], column[TARGETS:WIDE, :]
    right_g, right_h = all_g - left_g, all_h - left_h
    score = (
        left_g * left_g / (left_h + RIDGE)
        + right_g * right_g / (right_h + RIDGE)
        - all_g * all_g / (all_h + RIDGE)
    )
    share[z, 0:TARGETS, :] = -left_g / (left_h + RIDGE)
    share[z, TARGETS:SHARE, :] = jnp.broadcast_to(jnp.sum(score, axis=0, keepdims=True) * (1.0 / TARGETS), (8, LANES))

    def spread_line(slot, to, target):
        return remote(share.at[slot], share.at[slot], ssend_sem.at[to], srecv_sem.at[slot], target)

    for d in (4, 3, 5, 2, 6, 1, 7):
        to = (z + d) % NZ
        spread_line(z, to, device(0, y, x, to)).start()
    for d in (1, 7, 2, 6, 3, 5, 4):
        source = (z + d) % NZ
        spread_line(source, source, me).wait_recv()

    def pass_on(kind, slot, target, k):
        remote(
            pack.at[kind, slot], pack.at[kind, slot], psend_sem.at[kind, k], precv_sem.at[kind, slot], target
        ).start()

    def landed(kind, slot):
        remote(pack.at[kind, slot], pack.at[kind, slot], psend_sem.at[kind, 0], precv_sem.at[kind, slot], me).wait_recv()

    def write(src, kind, b, lanes):
        for a in range(4):
            for j in (0, 1):
                for n in (0, 1):
                    row = n * BINS + kind * 32 + b * 8 + a * 2 + j
                    weights_ref[pl.ds(pl.multiple_of(row * TARGETS, TARGETS), TARGETS), lanes] = src[
                        kind, b * 4 + a, pl.ds((j * 2 + n) * TARGETS, TARGETS), :
                    ]
        for n in (0, 1):
            rows8 = [
                src[kind, b * 4 + a, pl.ds(4 * TARGETS + j * 2 + n, 1), :] for a in range(4) for j in (0, 1)
            ]
            start = pl.multiple_of(n * BINS + kind * 32 + b * 8, 8)
            gains_ref[pl.ds(start, 8), lanes] = jnp.concatenate(rows8, axis=0)

    def to_mate(kind, slot):
        remote(
            pack.at[kind, slot], mate.at[kind, slot], msend_sem.at[kind, slot], mrecv_sem.at[kind, slot], mate_id
        ).start()

    ways = (0, -1, 1, 2)

    def at(kind, i, k):
        a, b = place(kind)
        return step(b, ways[k] * sign) * 4 + step(a, ways[i] * sign)

    for kind in (0, 1):
        a, b = place(kind)
        slot = b * 4 + a
        for zh in range(4):
            pack[kind, slot, pl.ds(zh * TARGETS, TARGETS), :] = share[kind * 4 + zh, 0:TARGETS, :]
            pack[kind, slot, pl.ds(4 * TARGETS + zh, 1), :] = share[kind * 4 + zh, TARGETS : TARGETS + 1, :]
            pack[kind, slot, pl.ds(4 * TARGETS + 4 + zh, 1), :] = share[kind * 4 + zh, TARGETS : TARGETS + 1, :]
        pass_on(kind, slot, device(kind, step(a, 2), b, z), 2)
        pass_on(kind, slot, device(kind, step(a, sign), b, z), 0)
        pass_on(kind, slot, device(kind, step(a, -sign), b, z), 1)

    def across(kind, i):
        a, b = place(kind)
        slot = at(kind, i, 0)
        if i == 3:
            pass_on(kind, slot, device(kind, a, step(b, 2), z), 14)
        pass_on(kind, slot, device(kind, a, step(b, sign), z), 3 + 2 * i)
        pass_on(kind, slot, device(kind, a, step(b, -sign), z), 4 + 2 * i)
        to_mate(kind, slot)

    def onward(i):
        for kind in (0, 1):
            landed(kind, at(kind, i, 1))
            a, b = place(kind)
            pass_on(kind, at(kind, i, 1), device(kind, a, step(b, sign), z), 11 + i)
            to_mate(kind, at(kind, i, 1))

    for kind in (0, 1):
        across(kind, 0)
    for i in (1, 2, 3):
        for kind in (0, 1):
            landed(kind, at(kind, i, 0))
            across(kind, i)
        if i == 2:
            onward(0)
    onward(1)
    onward(2)
    for i, k in ((0, 2), (0, 3), (1, 2), (2, 2), (3, 1), (3, 2), (1, 3), (2, 3), (3, 3)):
        for kind in (0, 1):
            landed(kind, at(kind, i, k))
            to_mate(kind, at(kind, i, k))

    def finish(b, carry):
        for kind in (0, 1):
            write(pack, kind, b, own_lanes)
        return carry

    lax.fori_loop(0, 4, finish, 0)

    def finish_mate(b, carry):
        for kind in (0, 1):
            for a in range(4):
                slot = b * 4 + a
                remote(
                    mate.at[kind, slot], mate.at[kind, slot], msend_sem.at[kind, slot], mrecv_sem.at[kind, slot], me
                ).wait_recv()
            write(mate, kind, b, mate_lanes)
        return carry

    lax.fori_loop(0, 4, finish_mate, 0)

    swap_bins.wait_send()
    swap_vals.wait_send()
    for kind in (0, 1):
        a, b = place(kind)
        for d in (1, 2, 3):
            tl_copy(kind, b, step(b, d)).wait_send()
    for d in range(1, NZ):
        to = (z + d) % NZ
        tz_copy(z, to).wait_send()
        spread_line(z, to, me).wait_send()
        if d % 2 == 0:
            line(to).wait_send()
        else:

            @pl.when(wide(to))
            def _(to=to):
                line(to).wait_send()

    def drain(m, carry):
        for kind in (0, 1):
            one(m, kind, me).wait_send()
            zero(m, kind, me).wait_send()
            remote(pack.at[kind, 0], pack.at[kind, 0], psend_sem.at[kind, m], precv_sem.at[kind, 0], me).wait_send()
        return carry

    lax.fori_loop(0, 15, drain, 0)

    def drain_pairs(m, carry):
        for kind in (0, 1):
            pair(m, kind).wait_send()
            remote(
                pack.at[kind, m], pack.at[kind, m], msend_sem.at[kind, m], mrecv_sem.at[kind, m], me
            ).wait_send()
        return carry

    lax.fori_loop(0, PLANE, drain_pairs, 0)


def on_device(bin_index, node_ids, gradients, hessians):
    rows, features = bin_index.shape
    dma = pltpu.SemaphoreType.DMA
    vmem = pltpu.VMEM
    f32 = jnp.float32
    whole = pl.BlockSpec(memory_space=pltpu.VMEM)
    operands = [bin_index, node_ids.reshape(1, rows), gradients.T, hessians.T]
    weights, gains = pl.pallas_call(
        functools.partial(kernel, rows),
        out_shape=(
            jax.ShapeDtypeStruct((2 * BINS * TARGETS, features), f32),
            jax.ShapeDtypeStruct((2 * BINS, features), f32),
        ),
        in_specs=[pl.BlockSpec(memory_space=pltpu.HBM)] * 4,
        out_specs=(whole, whole),
        scratch_shapes=[
            vmem((1, rows), jnp.int32),
            vmem((TARGETS, rows), jnp.bfloat16),
            vmem((TARGETS, rows), jnp.bfloat16),
            vmem((2 * rows, LANES), jnp.int32),
            vmem((2 * WIDE, 2 * rows), jnp.bfloat16),
            vmem((PIECE, rows), f32),
            vmem((PIECE, rows), f32),
            vmem((EARLY, 2 * WIDE, 4 * LANES), f32),
            vmem((NZ, 8, LANES), f32),
            vmem((2, 4, 8, LANES), f32),
            vmem((4, 2, 2 * WIDE, LANES), f32),
            vmem((16, 2, 2, WIDE, LANES), f32),
            vmem((16, 2, WIDE, LANES), f32),
            vmem((15, 2, 2 * WIDE, LANES), f32),
            vmem((15, 2, 2 * WIDE, LANES), f32),
            vmem((15, 2, WIDE, LANES), f32),
            vmem((15, 2, WIDE, LANES), f32),
            vmem((NZ, WIDE, LANES), f32),
            vmem((NZ, WIDE, LANES), f32),
            vmem((NZ, SHARE, LANES), f32),
            vmem((2, PLANE, PACK, LANES), f32),
            vmem((2, PLANE, PACK, LANES), f32),
            dma((4,)),
            dma((2,)),
            dma((2,)),
            dma((NZ,)),
            dma((NZ,)),
            dma((2, 4)),
            dma((2, 4)),
            dma((16, 2)),
            dma((16, 2)),
            dma((15, 2)),
            dma((15, 2)),
            dma((15, 2)),
            dma((15, 2)),
            dma((NZ,)),
            dma((NZ,)),
            dma((NZ,)),
            dma((NZ,)),
            dma((2, 15)),
            dma((2, PLANE)),
            dma((2, PLANE)),
            dma((2, PLANE)),
        ],
        compiler_params=pltpu.CompilerParams(collective_id=0, has_side_effects=True, vmem_limit_bytes=30 << 20),
        name="level",
    )(*[pltpu.with_memory_space_constraint(v, pltpu.HBM) for v in operands])
    weights = jnp.transpose(weights.reshape(2, BINS, TARGETS, features), (3, 0, 1, 2))
    gains = jnp.transpose(gains.reshape(2, BINS, features), (2, 0, 1))
    return (gains, weights)


def solution(mesh):
    return jax.shard_map(
        on_device,
        mesh=mesh,
        in_specs=(P("dp", None), P("dp"), P("dp", None), P("dp", None)),
        out_specs=(P(), P()),
        check_vma=False,
    )
```

time: 85.4 us -> 72.8 us (0.85)
  Pallas kernels: 78.2 us -> 69.4 us
  local copies, waits for them, and re-layouts: 6.36 us -> 2.67 us
    pallas_call x1, Pallas kernels: 78.2 us -> 69.4 us  [on_device(): pl.pallas_call(functools.partial(kernel, rows), out_shape=(jax.ShapeDtype...]
    unnamed x2, local copies, waits for them, and re-layouts: 6.36 us -> 2.67 us
where the time goes in v2:
time: 72.8 us; the launch traced here: 72.7 us
  Pallas kernels  69.4 us (95%)
  local copies, waits for them, and re-layouts  2.67 us (4%)
    pallas_call x1, Pallas kernels, on_device(): pl.pallas_call(functools.partial(kernel, rows), out_shape=(jax.ShapeDtype...  69.4 us
    unnamed x2, local copies, waits for them, and re-layouts  2.67 us

profile of v2, /device:TPU:1, one launch (start us, length us, event | category | flops | bytes accessed | tf_op | source)
XLA Modules:
  0.0 72.7 jit_solution(17934571318456651278)
XLA Ops:
  0.6 69.4 %level.1 = (f32[4096,256]{1,0:T(8,128)S(1)}, f32[128,256]{1,0:T(8,128)S(1)}) custom-call(s32[2048,256]{1,0:T(8,128)} %bins_hbm.1, s32[1,2048]{1,0:T(1,128)} %bitcast.13, bf16[32,2048]{1,0:T(8,128)(2,1)} %bitcast.11, bf16[32,2048]{1,0:T(8,128)(2,1)} %bitcast.12), custom_call_target="tpu_custom_call" | custom-call | tf_op jit(solution)/shard_map/level/pallas_call | solution.py:518
  70.0 0.7 copy.8
  70.7 2.0 %copy.9 = f32[256,2,64,32]{0,3,2,1:T(8,128)} copy(f32[256,2,64,32]{0,3,2,1:T(8,128)S(1)} %bitcast.9) | data formatting | bytes 8388608

commit v3 on v2

--- a/solution.py
+++ b/solution.py
@@ -18,8 +18,7 @@
 RIDGE = 1.0
 DEPTH = 1024
 PIECE = WIDE + 8
-EARLY = 3
-LAG = 3
+EARLY = 4
 SHARE = TARGETS + 8
 PACK = 4 * TARGETS + 8
 
@@ -148,8 +147,7 @@
             part = jnp.where(which == float(n), both, 0.0)
             spread[n * WIDE : (n + 1) * WIDE, start : start + rows] = part.astype(jnp.bfloat16)
 
-    def local(i, low, high):
-        t, u = i // 4, i % 4
+    def local(t, u, low, high):
         firsts = []
         for kind in (0, 1):
             a, b = place(kind)
@@ -224,92 +222,101 @@
 
     toward = (1, -1, 1)
 
-    def extras(i):
-        t, u = i // 4, i % 4
+    def extras(t, u):
         if t < 2:
             return []
         if t == 2:
             return [u]
-        return [4 + u, 8 + u] + ([12] if u == 2 else []) + ([13, 14] if u == 3 else [])
-
-    def target_of(i, kind):
-        t, u = i // 4, i % 4
+        return [4 + u, 8 + u] + {2: [12], 3: [13, 14]}.get(u, [])
+
+    def target_of(t, u, kind):
         a, b = place(kind)
         if t < 3:
             return device(kind, a, step(b, toward[t] * sign), z)
         return device(kind, step(a, toward[u] * sign), b, z)
 
-    def put1(i, kind, value):
-        for e in extras(i):
+    def put1(t, u, kind, value):
+        i = t * 4 + u
+        last = t == 3 and u == 3
+        for e in extras(t, u):
             one(e, kind, me).wait_recv()
             value = value + got1[e, kind]
-        if i == 15:
+        if last:
             for n in (0, 1):
                 zsent[kind * 4 + 2 + n] = value[n * WIDE : (n + 1) * WIDE, :]
         else:
             sent1[i, kind] = value
-            one(i, kind, target_of(i, kind)).start()
-
-    def put0(i):
+            one(i, kind, target_of(t, u, kind)).start()
+
+    def put0(t, u):
+        i = t * 4 + u
+        last = t == 3 and u == 3
         for kind in (0, 1):
             pair(i, kind).wait_recv()
             value = pairs[i, kind, h] + paired[i, kind]
-            for e in extras(i):
+            for e in extras(t, u):
                 zero(e, kind, me).wait_recv()
                 value = value + got0[e, kind]
-            if i == 15:
+            if last:
                 zsent[kind * 4 + h] = value
             else:
                 sent0[i, kind] = value
-                zero(i, kind, target_of(i, kind)).start()
-
-    def late1(i):
-        for kind in (0, 1):
-            put1(i, kind, raw[i - 12, kind])
-
-    def take(i, total):
+                zero(i, kind, target_of(t, u, kind)).start()
+
+    def late1(u):
+        for kind in (0, 1):
+            put1(3, u, kind, raw[u, kind])
+
+    def take(t, u, total):
+        i = t * 4 + u
         for kind in (0, 1):
             first = total[:, 2 * kind * LANES : (2 * kind + 1) * LANES]
             pairs[i, kind, 0] = first[0:WIDE, :]
             pairs[i, kind, 1] = first[WIDE : 2 * WIDE, :]
             pair(i, kind).start()
             second = total[:, (2 * kind + 1) * LANES : (2 * kind + 2) * LANES]
-            if i < 12:
-                put1(i, kind, second)
+            if t < 3:
+                put1(t, u, kind, second)
             else:
-                raw[i - 12, kind] = second
+                raw[u, kind] = second
 
     fill(mine, 0)
     loads[3].wait()
-    for i in range(EARLY):
-        early[i] = local(i, 0, rows)
+    def begin(u, carry):
+        early[u] = local(0, u, 0, rows)
+        return carry
+
+    lax.fori_loop(0, EARLY, begin, 0)
     swap_vals.wait_recv()
     fill(theirs, rows)
     swap_bins.wait_recv()
 
-    for i in range(16):
-        if i < EARLY:
-            take(i, early[i] + local(i, rows, 2 * rows))
-        else:
-            take(i, local(i, 0, 2 * rows))
-        if i == 1:
+    for t in range(4):
+
+        def stage(u, carry, t=t):
+            if t == 0:
+                take(0, u, early[u] + local(0, u, rows, 2 * rows))
+            else:
+                take(t, u, local(t, u, 0, 2 * rows))
+                put0(t - 1, u)
+            return carry
+
+        lax.fori_loop(0, 3 if t == 3 else 4, stage, 0)
+        if t == 0:
             totals_begin()
-        if i == 5:
+        if t == 2:
             totals_send(0, totals_z())
-        if i == 9:
-            totals_send(1, totals_line(0))
-        if LAG <= i:
-            if i - LAG < 12:
-                put0(i - LAG)
-        if i == 13:
-            late1(12)
-        if i == 14:
-            late1(13)
-    put0(12)
-    late1(14)
-    put0(13)
-    put0(14)
-    late1(15)
+
+    late1(0)
+    take(3, 3, local(3, 3, 0, 2 * rows))
+    late1(1)
+    put0(2, 3)
+    put0(3, 0)
+    late1(2)
+    put0(3, 1)
+    totals_send(1, totals_line(0))
+    put0(3, 2)
+    late1(3)
 
     def line(to):
         return remote(zsent.at[to], zgot.at[z], zsend.at[to], zrecv.at[z], device(0, y, x, to))
@@ -324,7 +331,7 @@
         def _(to=to):
             line(to).start()
 
-    put0(15)
+    put0(3, 3)
     for d in (4, 2, 6):
         to = (z + d) % NZ
 
@@ -416,9 +423,9 @@
             pack[kind, slot, pl.ds(zh * TARGETS, TARGETS), :] = share[kind * 4 + zh, 0:TARGETS, :]
             pack[kind, slot, pl.ds(4 * TARGETS + zh, 1), :] = share[kind * 4 + zh, TARGETS : TARGETS + 1, :]
             pack[kind, slot, pl.ds(4 * TARGETS + 4 + zh, 1), :] = share[kind * 4 + zh, TARGETS : TARGETS + 1, :]
-        pass_on(kind, slot, device(kind, step(a, 2), b, z), 2)
         pass_on(kind, slot, device(kind, step(a, sign), b, z), 0)
         pass_on(kind, slot, device(kind, step(a, -sign), b, z), 1)
+        pass_on(kind, slot, device(kind, step(a, 2), b, z), 2)
 
     def across(kind, i):
         a, b = place(kind)

time: 72.8 us -> 69.2 us (0.951)
  Pallas kernels: 69.4 us -> 65.8 us
    pallas_call x1, Pallas kernels: 69.4 us -> 65.8 us  [on_device(): pl.pallas_call(functools.partial(kernel, rows), out_shape=(jax.ShapeDtype...]
where the time goes in v3:
time: 69.2 us; the launch traced here: 69.1 us
  Pallas kernels  65.8 us (95%)
  local copies, waits for them, and re-layouts  2.67 us (4%)
    pallas_call x1, Pallas kernels, on_device(): pl.pallas_call(functools.partial(kernel, rows), out_shape=(jax.ShapeDtype...  65.8 us
    unnamed x2, local copies, waits for them, and re-layouts  2.67 us

profile of v3, /device:TPU:1, one launch (start us, length us, event | category | flops | bytes accessed | tf_op | source)
XLA Modules:
  0.0 69.1 jit_solution(17037790981699350490)
XLA Ops:
  0.6 65.8 %level.1 = (f32[4096,256]{1,0:T(8,128)S(1)}, f32[128,256]{1,0:T(8,128)S(1)}) custom-call(s32[2048,256]{1,0:T(8,128)} %bins_hbm.1, s32[1,2048]{1,0:T(1,128)} %bitcast.13, bf16[32,2048]{1,0:T(8,128)(2,1)} %bitcast.11, bf16[32,2048]{1,0:T(8,128)(2,1)} %bitcast.12), custom_call_target="tpu_custom_call" | custom-call | tf_op jit(solution)/shard_map/level/pallas_call | solution.py:525
  66.4 0.7 copy.8
  67.1 2.0 %copy.9 = f32[256,2,64,32]{0,3,2,1:T(8,128)} copy(f32[256,2,64,32]{0,3,2,1:T(8,128)S(1)} %bitcast.9) | data formatting | bytes 8388608

commit v4 on v3

--- a/solution.py
+++ b/solution.py
@@ -301,15 +301,17 @@
                 put0(t - 1, u)
             return carry
 
-        lax.fori_loop(0, 3 if t == 3 else 4, stage, 0)
+        lax.fori_loop(0, 2 if t == 3 else 4, stage, 0)
         if t == 0:
             totals_begin()
         if t == 2:
             totals_send(0, totals_z())
 
     late1(0)
+    take(3, 2, local(3, 2, 0, 2 * rows))
+    put0(2, 2)
+    late1(1)
     take(3, 3, local(3, 3, 0, 2 * rows))
-    late1(1)
     put0(2, 3)
     put0(3, 0)
     late1(2)

time: 69.2 us -> 69.2 us (level)
  no operation moved by 1% of the time
where the time goes in v4:
time: 69.2 us; the launch traced here: 69.1 us
  Pallas kernels  65.8 us (95%)
  local copies, waits for them, and re-layouts  2.67 us (4%)
    pallas_call x1, Pallas kernels, on_device(): pl.pallas_call(functools.partial(kernel, rows), out_shape=(jax.ShapeDtype...  65.8 us
    unnamed x2, local copies, waits for them, and re-layouts  2.67 us

profile of v4, /device:TPU:1, one launch (start us, length us, event | category | flops | bytes accessed | tf_op | source)
XLA Modules:
  0.0 69.1 jit_solution(16572718630670106495)
XLA Ops:
  0.6 65.8 %level.1 = (f32[4096,256]{1,0:T(8,128)S(1)}, f32[128,256]{1,0:T(8,128)S(1)}) custom-call(s32[2048,256]{1,0:T(8,128)} %bins_hbm.1, s32[1,2048]{1,0:T(1,128)} %bitcast.13, bf16[32,2048]{1,0:T(8,128)(2,1)} %bitcast.11, bf16[32,2048]{1,0:T(8,128)(2,1)} %bitcast.12), custom_call_target="tpu_custom_call" | custom-call | tf_op jit(solution)/shard_map/level/pallas_call | solution.py:527
  66.4 0.7 copy.8
  67.1 2.0 %copy.9 = f32[256,2,64,32]{0,3,2,1:T(8,128)} copy(f32[256,2,64,32]{0,3,2,1:T(8,128)S(1)} %bitcast.9) | data formatting | bytes 8388608
